TPU v7x, 512 devices: a whole 4x8x8 slice. The times are simulated.
512 devices in a mesh: img: 8 (over y_lo, core), cin: 8 (over x, y_hi), cout: 8 (over z).
Axes of the slice: x: 4, y: 8 (y_hi: 2, y_lo: 4; y = y_hi * 4 + y_lo), z: 8, core: 2. Of those that a mesh axis runs over, the one named last changes fastest.
Arguments:
- maps: bfloat16 [2, 8, 14, 14, 1024], P(None, 'img'), may hold values from -6 to 6
- w_first: bfloat16 [3, 3, 1024, 1024], P(None, None, 'cin', 'cout'), may hold values from -0.09375 to 0.09375
- w_reduce: bfloat16 [3, 3, 1024, 8192], P(None, None, 'img', ('cin', 'cout')), may hold values from -0.09375 to 0.09375
- w_wide: bfloat16 [3, 3, 8192, 8192], P(None, None, 'cin', ('img', 'cout')), may hold values from -0.03125 to 0.03125
Outputs:
- wide_out: bfloat16 [2, 8, 7, 7, 8192], P(None, 'cin', None, None, ('img', 'cout'))
All inputs are finite; a program needn't handle non-finite values.
Results may differ from a plain program's by a relative error of at most 0.014.
Values may be sent and summed in bfloat16 or wider, within the bound.
No kernel may reach another device: no remote copies, remote signals or barrier semaphores. Data moves between devices by JAX's collectives and lax.ppermute only.
A program may use at most 64 MiB of HBM per device.

v0:
```python
import jax
import jax.numpy as jnp
from jax import lax
from jax.sharding import PartitionSpec as P


def conv_block(padded, weight_flat, size, step):
    channels = padded.shape[3]
    windows = []
    for row_tap in range(3):
        for col_tap in range(3):
            windows.append(
                padded[
                    :,
                    row_tap : row_tap + step * (size - 1) + 1 : step,
                    col_tap : col_tap + step * (size - 1) + 1 : step,
                    :,
                ]
            )
    table = jnp.concatenate(windows, axis=3).reshape(-1, 9 * channels)
    total = jnp.dot(table, weight_flat, preferred_element_type=jnp.float32)
    return total.reshape(padded.shape[0], size, size, weight_flat.shape[1])


def conv_taps(padded, weight, size, step):
    count = padded.shape[0]
    channels = padded.shape[3]
    weight_flat = weight.reshape(9 * channels, weight.shape[3])
    group = 1
    for trial in range(1, 9):
        if count % trial == 0:
            group = trial
    blocks = padded.reshape(count // group, group, padded.shape[1], padded.shape[2], channels)
    results = lax.map(lambda block: conv_block(block, weight_flat, size, step), blocks)
    return results.reshape(count, size, size, weight.shape[3])


def pad_map(values):
    return jnp.pad(values, ((0, 0), (1, 1), (1, 1), (0, 0)))


def local(maps, w_first, w_reduce, w_wide):
    batches = maps.shape[0]
    side = maps.shape[2]
    half = side // 2
    in_block = w_first.shape[2]
    out_block = w_first.shape[3]
    flat = maps.reshape(-1, side, side, maps.shape[4])
    in_part = lax.dynamic_slice_in_dim(flat, lax.axis_index("cin") * in_block, in_block, 3)
    first_terms = conv_taps(pad_map(jnp.maximum(in_part, 0)), w_first, side, 1)
    first_terms = first_terms.reshape(batches, maps.shape[1], side, side, out_block)
    summed = lax.psum(first_terms, "cin")
    own_part = lax.dynamic_slice_in_dim(maps, lax.axis_index("cout") * out_block, out_block, 4)
    segment_maps = (own_part.astype(jnp.float32) + summed).astype(jnp.bfloat16)
    whole = lax.all_gather(segment_maps, "cout", axis=4, tiled=True)
    by_channel = lax.all_to_all(whole, "img", split_axis=4, concat_axis=1, tiled=True)
    images = by_channel.shape[1]
    rect_segment = jnp.maximum(by_channel, 0).reshape(-1, side, side, by_channel.shape[4])
    reduced = conv_taps(pad_map(rect_segment), w_reduce, half, 2).reshape(
        batches, images, half, half, w_reduce.shape[3]
    )
    out_width = w_wide.shape[3]
    summed_wide = lax.psum(reduced, "img")
    narrow = jnp.maximum(summed_wide, 0.0).astype(jnp.bfloat16)
    gathered = lax.all_gather(narrow, "cout", axis=4, tiled=True)
    flat_all = gathered.reshape(-1, half, half, gathered.shape[4])
    partial_value = conv_taps(pad_map(flat_all), w_wide, half, 1)
    partial_value = partial_value.reshape(batches, images, half, half, out_width)
    result = lax.psum_scatter(
        partial_value.astype(jnp.bfloat16), "cin", scatter_dimension=1, tiled=True
    )
    return result


def solution(mesh):
    in_specs = (
        P(None, "img", None, None, None),
        P(None, None, "cin", "cout"),
        P(None, None, "img", ("cin", "cout")),
        P(None, None, "cin", ("img", "cout")),
    )
    out_specs = P(None, "cin", None, None, ("img", "cout"))
    return jax.shard_map(local, mesh=mesh, in_specs=in_specs, out_specs=out_specs, check_vma=False)
```

profile of v0, /device:TPU:64, one launch (start us, length us, event | category | flops | bytes accessed | tf_op | source)
XLA Modules:
  0.0 461.7 jit_solution(14591765025077755233)
XLA Ops:
  6.5 1.1 constant_dynamic-slice_fusion.2
  7.8 0.1 slice_dynamic-update-slice_fusion.23
  7.8 0.1 slice_dynamic-update-slice_fusion.22
  8.0 0.1 slice_dynamic-update-slice_fusion.21
  8.0 0.1 slice_dynamic-update-slice_fusion.20
  8.1 0.1 slice_dynamic-update-slice_fusion.18
  8.2 1.1 convolution_bitcast_fusion.1
  9.3 116.6 %all-reduce.8.cloned.1.call-done = f32[2,1,14,14,128]{4,3,2,0,1:T(8,128)} async-done(((f32[2,1,14,14,128]{4,3,2,0,1:T(8,128)}), f32[2,1,14,14,128]{4,3,2,0,1:T(8,128)}) %all-reduce.8.cloned.1.call-update) | async-done | bytes 200720 | tf_op jit(solution)/shard_map/psum | solution.py:52
  126.0 1.0 add_convert_fusion
  126.9 26.5 %all_gather.6 = bf16[2,1,14,14,1024]{4,3,2,0,1:T(8,128)(2,1)S(1)} all-gather(bf16[2,1,14,14,128]{4,3,2,0,1:T(8,128)(2,1)S(1)} %add_convert_fusion), channel_id=1, replica_groups=mesh['img'=8,'cin'=8,'cout'=8] {'cout'}, dimensions={4}, use_global_device_ids=true | all-gather | bytes 903168 | tf_op jit(solution)/shard_map/all_gather | solution.py:55
  153.5 12.4 %copy.42 = bf16[2,1,14,14,1024]{3,0,2,1,4:T(2,128)(2,1)} copy(bf16[2,1,14,14,1024]{4,3,2,0,1:T(8,128)(2,1)S(1)} %all_gather.6) | data formatting | bytes 1605632 | tf_op jit(solution)/shard_map/all_gather | solution.py:55
  165.8 12.8 %reshape.68 = bf16[8,2,25088]{2,1,0:T(2,128)(2,1)} reshape(bf16[1024,1,14,2,14]{4,3,2,1,0:T(2,128)(2,1)} %bitcast.84) | data formatting | bytes 1605632
  178.7 3.5 all-to-all-start
  182.3 21.2 %all-to-all-done = bf16[8,2,25088]{2,1,0:T(2,128)(2,1)S(1)} async-done(((bf16[8,2,25088]{2,1,0:T(2,128)(2,1)}), bf16[8,2,25088]{2,1,0:T(2,128)(2,1)S(1)}, u32[]{:S(2)}, u32[]{:S(2)}) %all-to-all-start) | async-done | bytes 802848 | tf_op jit(solution)/shard_map/all_to_all | solution.py:56
  203.4 19.8 %reshape.69 = bf16[1024,1,14,2,14]{4,3,2,1,0:T(2,128)(2,1)} reshape(bf16[8,2,25088]{2,1,0:T(2,128)(2,1)S(1)} %all-to-all-done) | data formatting | bytes 1605632
  223.2 17.3 %copy.43 = bf16[2,1,14,14,1024]{4,0,3,2,1:T(2,128)(2,1)S(1)} copy(bf16[2,1,14,14,1024]{3,0,2,1,4:T(2,128)(2,1)} %bitcast.85) | data formatting | bytes 1605632 | tf_op jit(solution)/shard_map/all_to_all | solution.py:56
  240.5 0.7 broadcast_maximum_fusion
  241.2 0.5 max.33
  241.7 1.2 pad_bitcast_fusion.1
  242.9 4.0 while.26
  242.9 1.2 dynamic-slice_bitcast_fusion.6
  244.5 0.4 fusion.26
  245.0 1.1 dynamic-slice_bitcast_fusion.6
  246.4 0.4 fusion.26
  246.9 31.9 %all-reduce.11 = bf16[2,8,7,7,128]{4,1,0,3,2:T(8,128)(2,1)S(1)} all-reduce(f32[2,8,7,7,128]{4,1,0,3,2:T(8,128)S(1)} %get-tuple-element.61), channel_id=1, replica_groups=mesh['img'=8,'cin'=8,'cout'=8] {'img'}, use_global_device_ids=true, to_apply=%region_3.4 | all-reduce | flops 100352 | bytes 602112 | tf_op jit(solution)/shard_map/psum | solution.py:63
  278.8 0.7 maximum_convert_fusion
  279.6 41.6 %all-gather.2.cloned.1.call-done = bf16[2,8,7,7,1024]{4,1,0,3,2:T(8,128)(2,1)} async-done(((bf16[2,8,7,7,128]{4,1,0,3,2:T(8,128)(2,1)}), bf16[2,8,7,7,1024]{4,1,0,3,2:T(8,128)(2,1)}) %all-gather.2.cloned.1.call-update) | async-done | bytes 1605648 | tf_op jit(solution)/shard_map/all_gather | solution.py:65
  321.2 3.3 pad_bitcast_fusion
  324.5 17.2 %while.27 = (s32[]{:T(128)}, bf16[2,8,7,7,128]{4,0,3,2,1:T(2,128)(2,1)S(1)}, bf16[2,8,9,9,1024]{4,1,0,3,2:T(8,128)(2,1)}, bf16[9216,128]{1,0:T(8,128)(2,1)S(1)}) while((s32[]{:T(128)}, bf16[2,8,7,7,128]{4,0,3,2,1:T(2,128)(2,1)S(1)}, bf16[2,8,9,9,1024]{4,1,0,3,2:T(8,128)(2,1)}, bf16[9216,128]{1,0:T(8,128)(2,1)S(1)}) %tuple.60), condition=%wide.region_5.6_spmd.clone, body=%wide.region_4.5_spmd.sunk.clone | while | flops 924844032 | bytes 27191356 | solution.py:34
  324.5 1.4 dynamic-slice_bitcast_fusion.7
  326.0 0.1 slice_dynamic-update-slice_fusion.72
  326.1 0.1 slice_dynamic-update-slice_fusion.73
  326.3 0.1 slice_dynamic-update-slice_fusion.76
  326.3 0.1 slice_dynamic-update-slice_fusion.77
  326.5 2.0 fusion.29
  328.6 0.2 copy.72
  328.7 4.4 dynamic_update_slice.16
  333.1 1.4 dynamic-slice_bitcast_fusion.7
  334.7 0.1 slice_dynamic-update-slice_fusion.73
  334.8 0.1 slice_dynamic-update-slice_fusion.74
  334.9 0.1 slice_dynamic-update-slice_fusion.77
  335.1 2.0 fusion.29
  337.2 0.2 copy.72
  337.3 4.4 dynamic_update_slice.16
  341.8 0.7 copy-done.3
  342.5 1.3 dynamic-slice.2
  343.7 109.5 %all-reduce.10.cloned.1.call-done = bf16[2,8,7,7,128]{4,0,3,2,1:T(2,128)(2,1)} async-done(((bf16[2,8,7,7,128]{4,0,3,2,1:T(2,128)(2,1)}), bf16[2,8,7,7,128]{4,0,3,2,1:T(2,128)(2,1)}) %all-reduce.10.cloned.1.call-update) | async-done | bytes 200720
  453.3 1.9 constant_dynamic-slice_fusion
  (49 shorter events, 1.6 us)
Async XLA Ops:
  6.5 1.6 copy-start
  6.5 119.4 %all-reduce.8.cloned.1.call-start = ((), (), s32[]{:S(2)}) async-start(), calls=%async_computation.1 | async-start | bytes 458752 | tf_op jit(solution)/shard_map/psum | solution.py:52
  178.7 24.8 %all-to-all-start = ((bf16[8,2,25088]{2,1,0:T(2,128)(2,1)}), bf16[8,2,25088]{2,1,0:T(2,128)(2,1)S(1)}, u32[]{:S(2)}, u32[]{:S(2)}) async-start(bf16[8,2,25088]{2,1,0:T(2,128)(2,1)} %reshape.68), calls=%async_computation | async-start | bytes 1605632 | tf_op jit(solution)/shard_map/all_to_all | solution.py:56
  182.2 139.0 %all-gather.2.cloned.1.call-start = ((), (), s32[]{:S(2)}) async-start(), calls=%async_computation.2 | async-start | bytes 1806336 | tf_op jit(solution)/shard_map/all_gather | solution.py:65
  223.2 19.7 %copy-start.2 = (bf16[3,3,128,128]{3,2,1,0:T(8,128)(2,1)S(1)}, bf16[3,3,128,128]{3,2,1,0:T(8,128)(2,1)}, u32[]{:S(2)}) copy-start(bf16[3,3,128,128]{3,2,1,0:T(8,128)(2,1)} %param.10) | copy-start | bytes 884740
  242.9 81.6 %copy-start.1 = (bf16[3,3,1024,128]{3,2,1,0:T(8,128)(2,1)S(1)}, bf16[3,3,1024,128]{3,2,1,0:T(8,128)(2,1)}, u32[]{:S(2)}) copy-start(bf16[3,3,1024,128]{3,2,1,0:T(8,128)(2,1)} %param.11) | copy-start | bytes 7077892
  279.5 173.7 %all-reduce.10.cloned.1.call-start = ((), (), s32[]{:S(2)}) async-start(), calls=%async_computation.3 | async-start | bytes 401408
  341.8 0.7 copy-start.3
Sparse Core Ops, SparseCore 0:
  10.3 115.6 all-reduce.7
  279.6 41.5 all-gather.1
  342.6 110.6 all-reduce.9
where the time goes:
time: 463 us; the launch traced here: 462 us
  waiting for transfers between devices  289 us (62%)
  local copies, waits for them, and re-layouts  88.5 us (19%)
  blocking collectives  58.4 us (13%)
  between operations  13.3 us (3%)
  matrix products  6.06 us (1%)
    psum x1, waiting for transfers between devices, local(): summed = lax.psum(first_terms, 'cin')  117 us
    unnamed x4, waiting for transfers between devices  110 us
    all_gather x1, waiting for transfers between devices, local(): gathered = lax.all_gather(narrow, 'cout', axis=4, tiled=True)  41.6 us
    unnamed x19, local copies, waits for them, and re-layouts  36.8 us
    psum x1, blocking collectives, local(): summed_wide = lax.psum(reduced, 'img')  31.9 us
    all_gather x1, blocking collectives, local(): whole = lax.all_gather(segment_maps, 'cout', axis=4, tiled=True)  26.5 us
    all_to_all x1, waiting for transfers between devices, local(): lax.all_to_all(whole, 'img', split_axis=4, concat_axis=1, tiled=True)  21.2 us
    all_to_all x1, local copies, waits for them, and re-layouts, local(): lax.all_to_all(whole, 'img', split_axis=4, concat_axis=1, tiled=True)  17.3 us
  transfers between devices with their start and end apart: 4, of which 4 were waited for; matrix products, arithmetic and copies ran while one was open for 0% of the time, Pallas kernels for 0%

commit v1 on v0

--- a/solution.py
+++ b/solution.py
@@ -60,7 +60,7 @@
         batches, images, half, half, w_reduce.shape[3]
     )
     out_width = w_wide.shape[3]
-    summed_wide = lax.psum(reduced, "img")
+    summed_wide = jnp.sum(lax.all_gather(reduced, "img"), axis=0)
     narrow = jnp.maximum(summed_wide, 0.0).astype(jnp.bfloat16)
     gathered = lax.all_gather(narrow, "cout", axis=4, tiled=True)
     flat_all = gathered.reshape(-1, half, half, gathered.shape[4])

time: 463 us -> 478 us (1.032)
  waiting for transfers between devices: 289 us -> 336 us
  blocking collectives: 58.4 us -> 26.5 us
    all_gather x0 -> x1, waiting for transfers between devices: none -> 43.2 us  [local(): summed_wide = jnp.sum(lax.all_gather(reduced, 'img'), axis=0)]
    psum x1 -> x0, blocking collectives: 31.9 us -> none  [local(): summed_wide = lax.psum(reduced, 'img')]
    unnamed x19 -> x21, local copies, waits for them, and re-layouts: 36.8 us -> 37.6 us
    unnamed x4 -> x5, waiting for transfers between devices: 110 us -> 110 us
  transfers between devices with their start and end apart: 4 -> 5, of which waited for: 4 -> 5; matrix products, arithmetic and copies ran while one was open for 0% -> 0% of each run, Pallas kernels for 0% -> 0%
where the time goes in v1:
time: 478 us; the launch traced here: 477 us
  waiting for transfers between devices  336 us (70%)
  local copies, waits for them, and re-layouts  86.4 us (18%)
  blocking collectives  26.5 us (6%)
  between operations  13.3 us (3%)
  matrix products  6.06 us (1%)
    psum x1, waiting for transfers between devices, local(): summed = lax.psum(first_terms, 'cin')  117 us
    unnamed x5, waiting for transfers between devices  110 us
    all_gather x1, waiting for transfers between devices, local(): gathered = lax.all_gather(narrow, 'cout', axis=4, tiled=True)  45.4 us
    all_gather x1, waiting for transfers between devices, local(): summed_wide = jnp.sum(lax.all_gather(reduced, 'img'), axis=0)  43.2 us
    unnamed x21, local copies, waits for them, and re-layouts  37.6 us
    all_gather x1, blocking collectives, local(): whole = lax.all_gather(segment_maps, 'cout', axis=4, tiled=True)  26.5 us
    all_to_all x1, waiting for transfers between devices, local(): lax.all_to_all(whole, 'img', split_axis=4, concat_axis=1, tiled=True)  21.2 us
    all_to_all x1, local copies, waits for them, and re-layouts, local(): lax.all_to_all(whole, 'img', split_axis=4, concat_axis=1, tiled=True)  17.3 us
  transfers between devices with their start and end apart: 5, of which 5 were waited for; matrix products, arithmetic and copies ran while one was open for 0% of the time, Pallas kernels for 0%

profile of v1, /device:TPU:64, one launch (start us, length us, event | category | flops | bytes accessed | tf_op | source)
XLA Modules:
  0.0 476.8 jit_solution(7033032719916706997)
XLA Ops:
  6.5 1.1 constant_dynamic-slice_fusion.2
  7.8 0.1 slice_dynamic-update-slice_fusion.23
  7.8 0.1 slice_dynamic-update-slice_fusion.22
  8.0 0.1 slice_dynamic-update-slice_fusion.21
  8.0 0.1 slice_dynamic-update-slice_fusion.20
  8.1 0.1 slice_dynamic-update-slice_fusion.18
  8.2 1.1 convolution_bitcast_fusion.1
  9.4 116.6 %all-reduce.7.cloned.1.call-done = f32[2,1,14,14,128]{4,3,2,0,1:T(8,128)} async-done(((f32[2,1,14,14,128]{4,3,2,0,1:T(8,128)}), f32[2,1,14,14,128]{4,3,2,0,1:T(8,128)}) %all-reduce.7.cloned.1.call-update) | async-done | bytes 200720 | tf_op jit(solution)/shard_map/psum | solution.py:52
  126.0 1.0 add_convert_fusion
  126.9 26.5 %all_gather.9 = bf16[2,1,14,14,1024]{4,3,2,0,1:T(8,128)(2,1)S(1)} all-gather(bf16[2,1,14,14,128]{4,3,2,0,1:T(8,128)(2,1)S(1)} %add_convert_fusion), channel_id=1, replica_groups=mesh['img'=8,'cin'=8,'cout'=8] {'cout'}, dimensions={4}, use_global_device_ids=true | all-gather | bytes 903168 | tf_op jit(solution)/shard_map/all_gather | solution.py:55
  153.5 12.4 %copy.37 = bf16[2,1,14,14,1024]{3,0,2,1,4:T(2,128)(2,1)} copy(bf16[2,1,14,14,1024]{4,3,2,0,1:T(8,128)(2,1)S(1)} %all_gather.9) | data formatting | bytes 1605632 | tf_op jit(solution)/shard_map/all_gather | solution.py:55
  165.9 12.8 %reshape.69 = bf16[8,2,25088]{2,1,0:T(2,128)(2,1)} reshape(bf16[1024,1,14,2,14]{4,3,2,1,0:T(2,128)(2,1)} %bitcast.85) | data formatting | bytes 1605632
  178.7 3.5 all-to-all-start
  182.3 21.2 %all-to-all-done = bf16[8,2,25088]{2,1,0:T(2,128)(2,1)S(1)} async-done(((bf16[8,2,25088]{2,1,0:T(2,128)(2,1)}), bf16[8,2,25088]{2,1,0:T(2,128)(2,1)S(1)}, u32[]{:S(2)}, u32[]{:S(2)}) %all-to-all-start) | async-done | bytes 802848 | tf_op jit(solution)/shard_map/all_to_all | solution.py:56
  203.5 19.8 %reshape.70 = bf16[1024,1,14,2,14]{4,3,2,1,0:T(2,128)(2,1)} reshape(bf16[8,2,25088]{2,1,0:T(2,128)(2,1)S(1)} %all-to-all-done) | data formatting | bytes 1605632
  223.2 17.3 %copy.38 = bf16[2,1,14,14,1024]{4,0,3,2,1:T(2,128)(2,1)S(1)} copy(bf16[2,1,14,14,1024]{3,0,2,1,4:T(2,128)(2,1)} %bitcast.86) | data formatting | bytes 1605632 | tf_op jit(solution)/shard_map/all_to_all | solution.py:56
  240.5 0.7 broadcast_maximum_fusion
  241.2 0.5 max.33
  241.7 0.2 pad_bitcast_fusion.1
  242.0 1.9 while.26
  242.0 0.1 dynamic-slice_bitcast_fusion.6
  242.5 0.4 fusion.26
  242.9 0.1 dynamic-slice_bitcast_fusion.6
  243.4 0.4 fusion.26
  243.9 0.8 copy-done.3
  244.7 43.2 %all-gather.6.cloned.1.call-done = f32[16,8,7,7,128]{4,1,3,2,0:T(8,128)} async-done(((f32[2,8,7,7,128]{4,1,3,2,0:T(8,128)}), f32[16,8,7,7,128]{4,1,3,2,0:T(8,128)}) %all-gather.6.cloned.1.call-update) | async-done | bytes 3211280 | tf_op jit(solution)/shard_map/all_gather | solution.py:63
  287.9 2.1 reduce_sum.9
  290.0 0.7 maximum_convert_fusion
  290.8 45.4 %all-gather.4.cloned.1.call-done = bf16[2,8,7,7,1024]{4,1,3,2,0:T(8,128)(2,1)} async-done(((bf16[2,8,7,7,128]{4,1,3,2,0:T(8,128)(2,1)}), bf16[2,8,7,7,1024]{4,1,3,2,0:T(8,128)(2,1)}) %all-gather.4.cloned.1.call-update) | async-done | bytes 1605648 | tf_op jit(solution)/shard_map/all_gather | solution.py:65
  336.1 1.6 copy.63
  337.7 1.8 pad_bitcast_fusion
  339.5 17.2 %while.27 = (s32[]{:T(128)}, bf16[2,8,7,7,128]{4,0,3,2,1:T(2,128)(2,1)S(1)}, bf16[2,8,9,9,1024]{4,1,0,3,2:T(8,128)(2,1)}, bf16[9216,128]{1,0:T(8,128)(2,1)S(1)}) while((s32[]{:T(128)}, bf16[2,8,7,7,128]{4,0,3,2,1:T(2,128)(2,1)S(1)}, bf16[2,8,9,9,1024]{4,1,0,3,2:T(8,128)(2,1)}, bf16[9216,128]{1,0:T(8,128)(2,1)S(1)}) %tuple.62), condition=%wide.region_5.6_spmd.clone, body=%wide.region_4.5_spmd.sunk.clone | while | flops 924844032 | bytes 27191356 | solution.py:34
  339.5 1.4 dynamic-slice_bitcast_fusion.7
  341.1 0.1 slice_dynamic-update-slice_fusion.73
  341.1 0.1 slice_dynamic-update-slice_fusion.74
  341.3 0.1 slice_dynamic-update-slice_fusion.77
  341.4 0.1 slice_dynamic-update-slice_fusion.78
  341.5 2.0 fusion.29
  343.5 0.2 copy.66
  343.7 4.4 dynamic_update_slice.16
  348.1 1.4 dynamic-slice_bitcast_fusion.7
  350.1 2.0 fusion.29
  352.2 0.2 copy.66
  352.3 4.4 dynamic_update_slice.16
  356.8 0.7 copy-done.4
  357.5 1.3 dynamic-slice.2
  358.7 109.5 %all-reduce.9.cloned.1.call-done = bf16[2,8,7,7,128]{4,0,3,2,1:T(2,128)(2,1)} async-done(((bf16[2,8,7,7,128]{4,0,3,2,1:T(2,128)(2,1)}), bf16[2,8,7,7,128]{4,0,3,2,1:T(2,128)(2,1)}) %all-reduce.9.cloned.1.call-update) | async-done | bytes 200720
  468.2 2.0 constant_dynamic-slice_fusion
  (55 shorter events, 1.8 us)
Async XLA Ops:
  6.5 1.6 copy-start
  6.5 119.4 %all-reduce.7.cloned.1.call-start = ((), (), s32[]{:S(2)}) async-start(), calls=%async_computation.1 | async-start | bytes 458752 | tf_op jit(solution)/shard_map/psum | solution.py:52
  178.7 24.8 %all-to-all-start = ((bf16[8,2,25088]{2,1,0:T(2,128)(2,1)}), bf16[8,2,25088]{2,1,0:T(2,128)(2,1)S(1)}, u32[]{:S(2)}, u32[]{:S(2)}) async-start(bf16[8,2,25088]{2,1,0:T(2,128)(2,1)} %reshape.69), calls=%async_computation | async-start | bytes 1605632 | tf_op jit(solution)/shard_map/all_to_all | solution.py:56
  182.2 105.7 %all-gather.6.cloned.1.call-start = ((), (), s32[]{:S(2)}) async-start(), calls=%async_computation.3 | async-start | bytes 3612672 | tf_op jit(solution)/shard_map/all_gather | solution.py:63
  223.2 18.7 %copy-start.2 = (bf16[3,3,128,128]{3,2,1,0:T(8,128)(2,1)S(1)}, bf16[3,3,128,128]{3,2,1,0:T(8,128)(2,1)}, u32[]{:S(2)}) copy-start(bf16[3,3,128,128]{3,2,1,0:T(8,128)(2,1)} %param.10) | copy-start | bytes 884740
  243.8 0.8 copy-start.3
  243.9 95.7 %copy-start.1 = (bf16[3,3,1024,128]{3,2,1,0:T(8,128)(2,1)S(1)}, bf16[3,3,1024,128]{3,2,1,0:T(8,128)(2,1)}, u32[]{:S(2)}) copy-start(bf16[3,3,1024,128]{3,2,1,0:T(8,128)(2,1)} %param.11) | copy-start | bytes 7077892
  244.6 91.5 %all-gather.4.cloned.1.call-start = ((), (), s32[]{:S(2)}) async-start(), calls=%async_computation.2 | async-start | bytes 1806336 | tf_op jit(solution)/shard_map/all_gather | solution.py:65
  290.7 177.5 %all-reduce.9.cloned.1.call-start = ((), (), s32[]{:S(2)}) async-start(), calls=%async_computation.4 | async-start | bytes 401408
  356.7 0.7 copy-start.4
Sparse Core Ops, SparseCore 0:
  10.3 115.6 all-reduce.6
  244.8 43.0 all-gather.5
  290.8 45.2 all-gather.3
  357.6 110.6 all-reduce.8
